TPU v7x, 32 devices: a whole 2x2x4 slice. The times are simulated.
32 devices in a mesh: dp: 8 (over y, x, core), tensor: 4 (over z).
Axes of the slice: x: 2, y: 2, z: 4, core: 2. Of those that a mesh axis runs over, the one named last changes fastest.
Arguments:
- short_tokens: bfloat16 [16, 256, 768], P('dp'), may hold values from -6 to 6
- short_lengths: int32 [16], P('dp'), may hold values from 64 to 256, as said below
- long_tokens: bfloat16 [24, 512, 768], P('dp'), may hold values from -6 to 6
- long_lengths: int32 [24], P('dp'), may hold values from 257 to 512, as said below
- w_qkv: bfloat16 [3, 768, 768], P(None, None, 'tensor'), may hold values from -0.21875 to 0.21875
- b_qv: bfloat16 [2, 12, 64], P(None, 'tensor'), may hold values from -3 to 3
- w_out: bfloat16 [768, 768], P('tensor'), may hold values from -2.5 to 2.5
- res_biases: bfloat16 [2, 768], replicated, may hold values from -3 to 3
- ln_gains: bfloat16 [2, 768], replicated, may hold values from 0.099609375 to 1.8984375
- ln_shifts: bfloat16 [2, 768], replicated, may hold values from -3 to 3
- w_up: bfloat16 [768, 3072], P(None, 'tensor'), may hold values from -0.21875 to 0.21875
- b_up: bfloat16 [4, 768], P('tensor'), may hold values from -3 to 3
- w_down: bfloat16 [3072, 768], P('tensor'), may hold values from -0.109375 to 0.109375
- short_cotangent: bfloat16 [16, 256, 768], P('dp'), may hold values from -6 to 6
- long_cotangent: bfloat16 [24, 512, 768], P('dp'), may hold values from -6 to 6
Outputs:
- short_encoded: bfloat16 [16, 256, 768], P('dp')
- long_encoded: bfloat16 [24, 512, 768], P('dp')
- short_grad_tokens: float32 [16, 256, 768], P('dp')
- long_grad_tokens: float32 [24, 512, 768], P('dp')
- grad_qkv: float32 [3, 768, 768], P(None, 'dp', 'tensor')
- grad_qv_bias: float32 [2, 12, 64], P(None, 'tensor', 'dp')
- grad_out: float32 [768, 768], P('tensor', 'dp')
- grad_res_biases: float32 [2, 768], P(None, 'dp')
- grad_gains: float32 [2, 768], P(None, 'dp')
- grad_shifts: float32 [2, 768], P(None, 'dp')
- grad_up: float32 [768, 3072], P('dp', 'tensor')
- grad_up_bias: float32 [4, 768], P('tensor', 'dp')
- grad_down: float32 [3072, 768], P('tensor', 'dp')
Inputs may be any that keep to these rules, and one draw needn't show every extreme that they name: `short_lengths`: the first short pair has 256 valid tokens. `long_lengths`: the first long pair has 512 valid tokens.
All inputs are finite; a program needn't handle non-finite values.
Results may differ from a plain program's by a relative error of at most 0.013.
The roundings to bfloat16 on the way count: a program that leaves them out, or rounds other values in their place, can miss the bound.
Values sent between devices are 32-bit elements; how exact they have to be, the bound alone decides.
No kernel may reach another device: no remote copies, remote signals or barrier semaphores. Data moves between devices by JAX's collectives and lax.ppermute only.
A program may use at most 128 MiB of HBM per device.

v0:
```python
import jax
import jax.numpy as jnp
from jax import lax
from jax.sharding import PartitionSpec as P

HD = 64
EPSILON = 1e-12


def normalize(hidden):
    center = hidden - jnp.mean(hidden, -1, keepdims=True)
    factor = lax.rsqrt(jnp.mean(center * center, -1, keepdims=True) + EPSILON)
    return (center * factor, factor[:, 0])


def norm_back(upstream, normed, factor, gain):
    scaled = upstream * gain
    inner_mean = jnp.mean(scaled, -1, keepdims=True)
    cross_mean = jnp.mean(scaled * normed, -1, keepdims=True)
    return factor[:, None] * (scaled - inner_mean - normed * cross_mean)


def gelu_exact(inner):
    return jax.nn.gelu(inner, approximate=False)


def masked_scores(queries, key_rows, length):
    scores = jnp.einsum(
        "qhe,khe->hqk", queries, key_rows, preferred_element_type=jnp.float32
    ) * HD ** (-0.5)
    visible = jnp.arange(key_rows.shape[0]) < length
    return jnp.where(visible[None, None, :], scores, -1e30)


def attend(queries, key_rows, value_rows, length):
    scores = masked_scores(queries, key_rows, length)
    largest = jnp.max(scores, -1, keepdims=True)
    weights_exp = jnp.exp(scores - largest)
    total = jnp.sum(weights_exp, -1, keepdims=True)
    probs = weights_exp / total
    mixed = jnp.einsum(
        "hqk,khe->qhe", probs.astype(jnp.bfloat16), value_rows, preferred_element_type=jnp.float32
    )
    log_total = largest[..., 0] + jnp.log(total[..., 0])
    return (mixed.astype(jnp.bfloat16), log_total)


def attend_back(queries, key_rows, value_rows, length, log_total, grad_mixed):
    scores = masked_scores(queries, key_rows, length)
    probs = jnp.exp(scores - log_total[..., None])
    grad_values = jnp.einsum(
        "hqk,qhe->khe", probs.astype(jnp.bfloat16), grad_mixed, preferred_element_type=jnp.float32
    )
    grad_probs = jnp.einsum(
        "qhe,khe->hqk", grad_mixed, value_rows, preferred_element_type=jnp.float32
    )
    centered = jnp.sum(probs * grad_probs, -1, keepdims=True)
    grad_scores = (probs * (grad_probs - centered)).astype(jnp.bfloat16)
    grad_queries = jnp.einsum(
        "hqk,khe->qhe", grad_scores, key_rows, preferred_element_type=jnp.float32
    ) * HD ** (-0.5)
    grad_keys = jnp.einsum(
        "hqk,qhe->khe", grad_scores, queries, preferred_element_type=jnp.float32
    ) * HD ** (-0.5)
    return (grad_queries, grad_keys, grad_values)


def forward_pair(item_tuple):
    pair_q, pair_k, pair_v, length = item_tuple
    return attend(pair_q, pair_k, pair_v, length)


def backward_pair(item_tuple):
    pair_q, pair_k, pair_v, length, pair_lse, pair_grad = item_tuple
    return attend_back(pair_q, pair_k, pair_v, length, pair_lse, pair_grad)


def on_device(
    short_tokens,
    short_lengths,
    long_tokens,
    long_lengths,
    w_qkv,
    b_qv,
    w_out,
    res_biases,
    ln_gains,
    ln_shifts,
    w_up,
    b_up,
    w_down,
    short_cotangent,
    long_cotangent,
):
    short_pairs, short_slot, model_width = short_tokens.shape
    long_pairs, long_slot = (long_tokens.shape[0], long_tokens.shape[1])
    short_rows = short_pairs * short_slot
    long_rows = long_pairs * long_slot
    local_width = w_qkv.shape[2]
    heads_here = b_qv.shape[1]
    head_size = b_qv.shape[2]
    flat = jnp.concatenate(
        [
            short_tokens.reshape(short_rows, model_width),
            long_tokens.reshape(long_rows, model_width),
        ],
        0,
    )
    flat_float = flat.astype(jnp.float32)
    gain_rows = ln_gains.astype(jnp.float32)
    shift_rows = ln_shifts.astype(jnp.float32)
    bias_float = res_biases.astype(jnp.float32)
    projected = jnp.einsum("rd,cde->cre", flat, w_qkv, preferred_element_type=jnp.float32)
    bias_rows = jnp.stack(
        [
            b_qv[0].reshape(local_width).astype(jnp.float32),
            jnp.zeros((local_width,), jnp.float32),
            b_qv[1].reshape(local_width).astype(jnp.float32),
        ]
    )
    projected = (projected + bias_rows[:, None, :]).astype(jnp.bfloat16)
    short_proj = projected[:, :short_rows].reshape(
        3, short_pairs, short_slot, heads_here, head_size
    )
    long_proj = projected[:, short_rows:].reshape(3, long_pairs, long_slot, heads_here, head_size)
    short_att, short_lse = lax.map(
        forward_pair, (short_proj[0], short_proj[1], short_proj[2], short_lengths)
    )
    long_att, long_lse = lax.map(
        forward_pair, (long_proj[0], long_proj[1], long_proj[2], long_lengths)
    )
    mixed = jnp.concatenate(
        [short_att.reshape(short_rows, local_width), long_att.reshape(long_rows, local_width)], 0
    )
    attn_part = jnp.dot(mixed, w_out, preferred_element_type=jnp.float32)
    attn_total = lax.psum(attn_part, "tensor")
    normed_one, factor_one = normalize(flat_float + attn_total + bias_float[0])
    first_out = normed_one * gain_rows[0] + shift_rows[0]
    first_low = first_out.astype(jnp.bfloat16)
    inner = jnp.dot(first_low, w_up, preferred_element_type=jnp.float32) + b_up[0].astype(
        jnp.float32
    )
    activated = gelu_exact(inner).astype(jnp.bfloat16)
    ffn_part = jnp.dot(activated, w_down, preferred_element_type=jnp.float32)
    ffn_total = lax.psum(ffn_part, "tensor")
    normed_two, factor_two = normalize(first_out + ffn_total + bias_float[1])
    encoded = (normed_two * gain_rows[1] + shift_rows[1]).astype(jnp.bfloat16)
    upstream = jnp.concatenate(
        [
            short_cotangent.reshape(short_rows, model_width),
            long_cotangent.reshape(long_rows, model_width),
        ],
        0,
    ).astype(jnp.float32)
    grad_second = norm_back(upstream, normed_two, factor_two, gain_rows[1])
    small_second = jnp.stack(
        [jnp.sum(grad_second, 0), jnp.sum(upstream * normed_two, 0), jnp.sum(upstream, 0)]
    )
    grad_branch = grad_second.astype(jnp.bfloat16)
    grad_down = jnp.einsum("rf,rd->fd", activated, grad_branch, preferred_element_type=jnp.float32)
    grad_activated = jnp.einsum(
        "rd,fd->rf", grad_branch, w_down, preferred_element_type=jnp.float32
    )
    ignored_value, gelu_pullback = jax.vjp(gelu_exact, inner)
    grad_inner = gelu_pullback(grad_activated)[0].astype(jnp.bfloat16)
    grad_up = jnp.einsum("rd,rf->df", first_low, grad_inner, preferred_element_type=jnp.float32)
    grad_up_bias = jnp.sum(grad_inner.astype(jnp.float32), 0)[None, :]
    input_part = jnp.einsum("rf,df->rd", grad_inner, w_up, preferred_element_type=jnp.float32)
    up_shard, down_shard, up_bias_shard, small_second_shard = (
        lax.psum_scatter(grad_up, "dp", scatter_dimension=0, tiled=True),
        lax.psum_scatter(grad_down, "dp", scatter_dimension=1, tiled=True),
        lax.psum_scatter(grad_up_bias, "dp", scatter_dimension=1, tiled=True),
        lax.psum_scatter(small_second, "dp", scatter_dimension=1, tiled=True),
    )
    grad_first_out = grad_second + lax.psum(input_part, "tensor")
    grad_first = norm_back(grad_first_out, normed_one, factor_one, gain_rows[0])
    small_first = jnp.stack(
        [
            jnp.sum(grad_first, 0),
            jnp.sum(grad_first_out * normed_one, 0),
            jnp.sum(grad_first_out, 0),
        ]
    )
    grad_attn = grad_first.astype(jnp.bfloat16)
    grad_out = jnp.einsum("rl,rd->ld", mixed, grad_attn, preferred_element_type=jnp.float32)
    grad_mixed = jnp.einsum(
        "rd,ld->rl", grad_attn, w_out, preferred_element_type=jnp.float32
    ).astype(jnp.bfloat16)
    short_grad_mixed = grad_mixed[:short_rows].reshape(
        short_pairs, short_slot, heads_here, head_size
    )
    long_grad_mixed = grad_mixed[short_rows:].reshape(long_pairs, long_slot, heads_here, head_size)
    short_gq, short_gk, short_gv = lax.map(
        backward_pair,
        (short_proj[0], short_proj[1], short_proj[2], short_lengths, short_lse, short_grad_mixed),
    )
    long_gq, long_gk, long_gv = lax.map(
        backward_pair,
        (long_proj[0], long_proj[1], long_proj[2], long_lengths, long_lse, long_grad_mixed),
    )
    short_grads = (
        jnp.stack([short_gq, short_gk, short_gv])
        .astype(jnp.bfloat16)
        .reshape(3, short_rows, local_width)
    )
    long_grads = (
        jnp.stack([long_gq, long_gk, long_gv])
        .astype(jnp.bfloat16)
        .reshape(3, long_rows, local_width)
    )
    grad_projected = jnp.concatenate([short_grads, long_grads], 1)
    grad_qkv = jnp.einsum("rd,cre->cde", flat, grad_projected, preferred_element_type=jnp.float32)
    grad_bias_rows = jnp.sum(grad_projected.astype(jnp.float32), 1)
    grad_qv_bias = jnp.stack([grad_bias_rows[0], grad_bias_rows[2]]).reshape(
        2, heads_here, head_size
    )
    token_part = jnp.einsum(
        "cre,cde->rd", grad_projected, w_qkv, preferred_element_type=jnp.float32
    )
    qkv_shard, qv_bias_shard, out_shard, small_first_shard = (
        lax.psum_scatter(grad_qkv, "dp", scatter_dimension=1, tiled=True),
        lax.psum_scatter(grad_qv_bias, "dp", scatter_dimension=2, tiled=True),
        lax.psum_scatter(grad_out, "dp", scatter_dimension=1, tiled=True),
        lax.psum_scatter(small_first, "dp", scatter_dimension=1, tiled=True),
    )
    grad_tokens = grad_first + lax.psum(token_part, "tensor")
    grad_res_biases = jnp.concatenate([small_first_shard[0:1], small_second_shard[0:1]], 0)
    grad_gains = jnp.concatenate([small_first_shard[1:2], small_second_shard[1:2]], 0)
    grad_shifts = jnp.concatenate([small_first_shard[2:3], small_second_shard[2:3]], 0)
    return (
        encoded[:short_rows].reshape(short_pairs, short_slot, model_width),
        encoded[short_rows:].reshape(long_pairs, long_slot, model_width),
        grad_tokens[:short_rows].reshape(short_pairs, short_slot, model_width),
        grad_tokens[short_rows:].reshape(long_pairs, long_slot, model_width),
        qkv_shard,
        qv_bias_shard,
        out_shard,
        grad_res_biases,
        grad_gains,
        grad_shifts,
        up_shard,
        up_bias_shard,
        down_shard,
    )


def solution(mesh):
    return jax.shard_map(
        on_device,
        mesh=mesh,
        in_specs=(
            P("dp", None, None),
            P("dp"),
            P("dp", None, None),
            P("dp"),
            P(None, None, "tensor"),
            P(None, "tensor", None),
            P("tensor", None),
            P(),
            P(),
            P(),
            P(None, "tensor"),
            P("tensor", None),
            P("tensor", None),
            P("dp", None, None),
            P("dp", None, None),
        ),
        out_specs=(
            P("dp", None, None),
            P("dp", None, None),
            P("dp", None, None),
            P("dp", None, None),
            P(None, "dp", "tensor"),
            P(None, "tensor", "dp"),
            P("tensor", "dp"),
            P(None, "dp"),
            P(None, "dp"),
            P(None, "dp"),
            P("dp", "tensor"),
            P("tensor", "dp"),
            P("tensor", "dp"),
        ),
        check_vma=False,
    )
```

profile of v0, /device:TPU:0, one launch (start us, length us, event | category | flops | bytes accessed | tf_op | source)
XLA Modules:
  0.0 1305.4 jit_solution(6530653363544916583)
XLA Ops:
  21.0 15.0 %while.53 = (s32[]{:T(128)}, bf16[3,512,3,64]{1,3,2,0:T(8,128)(2,1)}, f32[3,3,512]{2,1,0:T(4,128)}, bf16[3,512,3,64]{1,3,2,0:T(8,128)(2,1)S(1)}, s32[3]{0:T(128)...) while((s32[]{:T(128)}, bf16[3,512,3,64]{1,3,2,0:T(8,128)(2,1)}, ...), condition=%wide.region_7.8_spmd, body=%wide.region_4.7_spmd.sunk | while | flops 210861056 | bytes 10283621 | solution.py:129
  43.2 5.3 while.52
  50.9 4.7 fusion.137
  58.1 223.2 %all-reduce.6.cloned.1.call-done = f32[2048,768]{1,0:T(8,128)} async-done(((f32[2048,768]{1,0:T(8,128)}), f32[2048,768]{1,0:T(8,128)}) %all-reduce.6.cloned.1.call-update) | async-done | bytes 6291472 | tf_op jit(solution)/shard_map/psum | solution.py:136
  281.3 4.2 fusion.130
  288.2 18.4 %multiply_convert_fusion.2 = (bf16[2048,768]{1,0:T(8,128)(2,1)S(1)}, f32[2048,768]{1,0:T(8,128)}, f32[2048,768]{1,0:T(8,128)}) fusion(f32[768]{0:T(1024)S(1)} %copy-done.32, bf16[2048,768]{1,0:T(8,128)(2,1)S(1)} %fusion.103, bf16[768,768]{1,0:T(8,128)(2,1)S(1)} %copy-done), kind=kOutput, calls=%fused_computation.132 | convolution fusion | flops 2519728128 | bytes 20057088 | tf_op jit(solution)/shard_map/dot_general | solution.py:140
  308.3 4.6 fusion.138
  313.1 221.7 %all-reduce.8.cloned.1.call-done = f32[2048,768]{1,0:T(8,128)} async-done(((f32[2048,768]{1,0:T(8,128)}), f32[2048,768]{1,0:T(8,128)}) %all-reduce.8.cloned.1.call-update) | async-done | bytes 6291472 | tf_op jit(solution)/shard_map/psum | solution.py:145
  534.8 5.7 fusion.128
  542.4 4.6 fusion.97
  547.0 5.8 fusion.126
  552.9 9.5 convert_reduce_fusion.1
  564.2 4.5 fusion.139
  571.6 219.0 %all-reduce.10.cloned.1.call-done = f32[2048,768]{1,0:T(8,128)} async-done(((f32[2048,768]{1,0:T(8,128)}), f32[2048,768]{1,0:T(8,128)}) %all-reduce.10.cloned.1.call-update) | async-done | bytes 6291472 | tf_op jit(solution)/shard_map/psum | solution.py:175
  790.6 8.1 multiply_reduce_fusion.2
  798.8 4.7 fusion.125
  811.8 25.9 %while.55 = (s32[]{:T(128)}, bf16[3,512,3,64]{1,3,2,0:T(8,128)(2,1)}, bf16[3,512,3,64]{1,3,2,0:T(8,128)(2,1)}, bf16[3,512,3,64]{1,3,2,0:T(8,128)(2,1)}, bf16[3,5...) while((s32[]{:T(128)}, ...), condition=%wide.region_24.25_spmd, body=%wide.region_22.24_spmd.sunk | while | flops 510589952 | bytes 35625200 | solution.py:197
  838.7 5.1 fusion.119
  844.2 9.6 while.54
  866.3 5.1 fusion.116
  871.4 4.3 copy.129
  875.7 4.7 reshape.242
  880.5 6.0 convolution_bitcast_fusion.1
  886.5 7.9 fusion.110
  894.8 7.0 fusion.140
  912.1 13.6 %all-reduce = f32[2,3,64]{2,1,0:T(4,128)S(1)} all-reduce(f32[2,3,64]{2,1,0:T(4,128)S(1)} %reshape.234), channel_id=3, replica_groups=mesh['dp'=8,'tensor'=4] {'dp'}, use_global_device_ids=true, to_apply=%region_28.29.clone | all-reduce | flops 384 | bytes 3072
  929.4 8.8 reduce-scatter.25.cloned.1.call-done
  939.8 42.0 %reduce-scatter.23.cloned.1.call-done = f32[96,576]{1,0:T(8,128)} async-done(((f32[768,576]{1,0:T(8,128)}), f32[96,576]{1,0:T(8,128)}) %reduce-scatter.23.cloned.1.call-update) | async-done | bytes 221200
  983.6 223.4 %all-reduce.12.cloned.1.call-done = f32[2048,768]{1,0:T(8,128)} async-done(((f32[2048,768]{1,0:T(8,128)}), f32[2048,768]{1,0:T(8,128)}) %all-reduce.12.cloned.1.call-update) | async-done | bytes 6291472 | tf_op jit(solution)/shard_map/psum | solution.py:226
  1207.0 5.5 add.175
  1216.2 35.8 %reduce-scatter.21.cloned.1.call-done = f32[768,96]{0,1:T(8,128)} async-done(((f32[768,768]{0,1:T(8,128)}), f32[768,96]{0,1:T(8,128)}) %reduce-scatter.21.cloned.1.call-update) | async-done | bytes 294928 | tf_op jit(solution)/shard_map/reduce_scatter | solution.py:171
  1252.0 46.3 %reduce-scatter.19.cloned.1.call-done = f32[96,768]{1,0:T(8,128)} async-done(((f32[768,768]{1,0:T(8,128)}), f32[96,768]{1,0:T(8,128)}) %reduce-scatter.19.cloned.1.call-update) | async-done | bytes 294928 | tf_op jit(solution)/shard_map/reduce_scatter | solution.py:170
  (326 shorter events, 135.1 us)
Async XLA Ops:
  7.2 281.0 %copy-start = (bf16[768,768]{1,0:T(8,128)(2,1)S(1)}, bf16[768,768]{1,0:T(8,128)(2,1)}, u32[]{:S(2)}) copy-start(bf16[768,768]{1,0:T(8,128)(2,1)} %param.33) | copy-start | bytes 3538948
  7.2 274.1 %all-reduce.6.cloned.1.call-start = ((), (), s32[]{:S(2)}) async-start(), calls=%async_computation.7 | async-start | bytes 12582912 | tf_op jit(solution)/shard_map/psum | solution.py:136
  12.8 8.1 copy-start.40
  21.0 20.5 %copy-start.16 = (bf16[1,512,192]{1,2,0:T(8,128)(2,1)S(1)}, bf16[1,512,192]{1,2,0:T(8,128)(2,1)}, u32[]{:S(2)}) copy-start(bf16[1,512,192]{1,2,0:T(8,128)(2,1)} %get-tuple-element.455) | copy-start | bytes 589828
  21.0 22.1 %copy-start.42 = (s32[2]{0:T(128)S(1)}, s32[2]{0:T(128)}, u32[]{:S(2)}) copy-start(s32[2]{0:T(128)} %param.24) | copy-start | bytes 28
  36.0 7.1 copy-start.6
  48.5 7.1 copy-start.23
  55.6 479.2 %all-reduce.8.cloned.1.call-start = ((), (), s32[]{:S(2)}) async-start(), calls=%async_computation.8 | async-start | bytes 12582912 | tf_op jit(solution)/shard_map/psum | solution.py:145
  288.2 18.5 %copy-start.9 = (bf16[2048,768]{1,0:T(8,128)(2,1)}, bf16[2048,768]{1,0:T(8,128)(2,1)S(1)}, u32[]{:S(2)}) copy-start(bf16[2048,768]{1,0:T(8,128)(2,1)S(1)} %fusion.103) | copy-start | bytes 9437188
  288.2 20.2 %copy-start.38 = (bf16[768,768]{1,0:T(8,128)(2,1)S(1)}, bf16[768,768]{1,0:T(8,128)(2,1)}, u32[]{:S(2)}) copy-start(bf16[768,768]{1,0:T(8,128)(2,1)} %param.35) | copy-start | bytes 3538948
  312.9 477.7 %all-reduce.10.cloned.1.call-start = ((), (), s32[]{:S(2)}) async-start(), calls=%async_computation.9 | async-start | bytes 12582912 | tf_op jit(solution)/shard_map/psum | solution.py:175
  542.4 10.5 slice-start.1
  552.9 9.5 copy-start.4
  568.7 221.9 %copy-start.22 = (f32[768]{0:T(1024)S(1)}, f32[768]{0:T(1024)}, u32[]{:S(2)}) copy-start(f32[768]{0:T(1024)} %get-tuple-element.469) | copy-start | bytes 9220
  568.7 339.6 %reduce-scatter.31.cloned.1.call-start = ((), (), s32[]{:S(2)}) async-start(), calls=%async_computation.17 | async-start | bytes 442368
  570.3 339.4 %reduce-scatter.29.cloned.1.call-start = ((), (), s32[]{:S(2)}) async-start(), calls=%async_computation.16 | async-start | bytes 442368
  571.4 355.0 %reduce-scatter.27.cloned.1.call-start = ((), (), s32[]{:S(2)}) async-start(), calls=%async_computation.15 | async-start | bytes 442368
  798.8 7.4 copy-start.12
  803.5 8.3 copy-start.41
  837.7 6.6 copy-start.11
  837.7 6.6 copy-start.24
  837.7 6.6 copy-start.43
  838.7 99.5 %reduce-scatter.25.cloned.1.call-start = ((), (), s32[]{:S(2)}) async-start(), calls=%async_computation.14 | async-start | bytes 884736
  843.9 137.8 %reduce-scatter.23.cloned.1.call-start = ((), (), s32[]{:S(2)}) async-start(), calls=%async_computation.13 | async-start | bytes 2211840
  853.8 12.5 copy-start.13
  871.4 9.0 copy-start.14
  871.4 9.0 copy-start.15
  880.4 326.6 %all-reduce.12.cloned.1.call-start = ((), (), s32[]{:S(2)}) async-start(), calls=%async_computation.10 | async-start | bytes 12582912 | tf_op jit(solution)/shard_map/psum | solution.py:226
  886.5 365.6 %reduce-scatter.21.cloned.1.call-start = ((), (), s32[]{:S(2)}) async-start(), calls=%async_computation.12 | async-start | bytes 2654208 | tf_op jit(solution)/shard_map/reduce_scatter | solution.py:171
  894.5 7.3 copy-start.44
  894.5 403.9 %reduce-scatter.19.cloned.1.call-start = ((), (), s32[]{:S(2)}) async-start(), calls=%async_computation.11 | async-start | bytes 2654208 | tf_op jit(solution)/shard_map/reduce_scatter | solution.py:170
  1207.0 91.4 %copy-start.1 = (bf16[768,768]{1,0:T(8,128)(2,1)S(1)}, bf16[768,768]{1,0:T(8,128)(2,1)}, u32[]{:S(2)}) copy-start(bf16[768,768]{1,0:T(8,128)(2,1)} %param.33) | copy-start | bytes 3538948
  (37 other events, 80.8 us)
Sparse Core Ops, SparseCore 0:
  55.7 225.5 all-reduce.5
  313.0 221.7 all-reduce.7
  568.9 221.7 all-reduce.9
  793.5 32.7 reduce-scatter.30
  829.3 33.8 reduce-scatter.28
  866.1 33.8 reduce-scatter.26
  903.2 34.9 reduce-scatter.24
  941.6 40.1 reduce-scatter.22
  984.1 222.8 all-reduce.11
  1210.8 41.2 reduce-scatter.20
  1256.0 42.3 reduce-scatter.18
where the time goes:
time: 1310 us
  waiting for transfers between devices  1020 us (78%)
  matrix products  109 us (8%)
  local copies, waits for them, and re-layouts  84.2 us (6%)
  other arithmetic  59.6 us (5%)
  between operations  15.9 us (1%)
  blocking collectives  13.6 us (1%)
    psum x1, waiting for transfers between devices, on_device(): grad_tokens = grad_first + lax.psum(token_part, 'tensor')  223 us
    psum x1, waiting for transfers between devices, on_device(): attn_total = lax.psum(attn_part, 'tensor')  223 us
    psum x1, waiting for transfers between devices, on_device(): ffn_total = lax.psum(ffn_part, 'tensor')  222 us
    psum x1, waiting for transfers between devices, on_device(): grad_first_out = grad_second + lax.psum(input_part, 'tensor')  219 us
    unnamed x16, waiting for transfers between devices  50.9 us
    reduce_scatter x1, waiting for transfers between devices, on_device(): lax.psum_scatter(grad_up, 'dp', scatter_dimension=0, tiled=True)  46.3 us
    reduce_scatter x1, waiting for transfers between devices, on_device(): lax.psum_scatter(grad_down, 'dp', scatter_dimension=1, tiled=True)  35.8 us
    unnamed x111, local copies, waits for them, and re-layouts  27.9 us
  transfers between devices with their start and end apart: 11, of which 8 were waited for; matrix products, arithmetic and copies ran while one was open for 10% of the time, Pallas kernels for 0%

commit v1 on v0

--- a/solution.py
+++ b/solution.py
@@ -133,7 +133,11 @@
         [short_att.reshape(short_rows, local_width), long_att.reshape(long_rows, local_width)], 0
     )
     attn_part = jnp.dot(mixed, w_out, preferred_element_type=jnp.float32)
-    attn_total = lax.psum(attn_part, "tensor")
+    attn_total = attn_part
+    for hop in (1, 2):
+        attn_total = attn_total + lax.ppermute(
+            attn_total, "tensor", [(dev, dev ^ hop) for dev in range(4)]
+        )
     normed_one, factor_one = normalize(flat_float + attn_total + bias_float[0])
     first_out = normed_one * gain_rows[0] + shift_rows[0]
     first_low = first_out.astype(jnp.bfloat16)

time: 1310 us -> 1500 us (1.15)
  waiting for transfers between devices: 1020 us -> 1210 us
    ppermute x0 -> x2, waiting for transfers between devices: none -> 405 us  [on_device(): lax.ppermute(attn_total, 'tensor', [(dev, dev ^ hop) for dev in range(4)])]
    psum x1 -> x0, waiting for transfers between devices: 223 us -> none  [on_device(): attn_total = lax.psum(attn_part, 'tensor')]
    unnamed x16 -> x15, waiting for transfers between devices: 50.9 us -> 52.4 us
  transfers between devices with their start and end apart: 11 -> 12, of which waited for: 8 -> 9; matrix products, arithmetic and copies ran while one was open for 10% -> 9% of each run, Pallas kernels for 0% -> 0%
where the time goes in v1:
time: 1500 us; the launch traced here: 1490 us
  waiting for transfers between devices  1210 us (81%)
  matrix products  106 us (7%)
  local copies, waits for them, and re-layouts  80.3 us (5%)
  other arithmetic  59.3 us (4%)
  between operations  16.2 us (1%)
    ppermute x2, waiting for transfers between devices, on_device(): lax.ppermute(attn_total, 'tensor', [(dev, dev ^ hop) for dev in range(4)])  405 us
    psum x1, waiting for transfers between devices, on_device(): ffn_total = lax.psum(ffn_part, 'tensor')  224 us
    psum x1, waiting for transfers between devices, on_device(): grad_tokens = grad_first + lax.psum(token_part, 'tensor')  223 us
    psum x1, waiting for transfers between devices, on_device(): grad_first_out = grad_second + lax.psum(input_part, 'tensor')  220 us
    unnamed x15, waiting for transfers between devices  52.4 us
    reduce_scatter x1, waiting for transfers between devices, on_device(): lax.psum_scatter(grad_up, 'dp', scatter_dimension=0, tiled=True)  46.2 us
    reduce_scatter x1, waiting for transfers between devices, on_device(): lax.psum_scatter(grad_down, 'dp', scatter_dimension=1, tiled=True)  36 us
  transfers between devices with their start and end apart: 12, of which 9 were waited for; matrix products, arithmetic and copies ran while one was open for 9% of the time, Pallas kernels for 0%

profile of v1, /device:TPU:0, one launch (start us, length us, event | category | flops | bytes accessed | tf_op | source)
XLA Modules:
  0.0 1489.8 jit_solution(8350951096529718978)
XLA Ops:
  8.3 4.1 fusion.122
  21.1 15.0 %while.53 = (s32[]{:T(128)}, bf16[3,512,3,64]{1,3,2,0:T(8,128)(2,1)}, f32[3,3,512]{2,1,0:T(4,128)}, bf16[3,512,3,64]{1,3,2,0:T(8,128)(2,1)S(1)}, s32[3]{0:T(128)...) while((s32[]{:T(128)}, bf16[3,512,3,64]{1,3,2,0:T(8,128)(2,1)}, ...), condition=%wide.region_7.8_spmd, body=%wide.region_4.7_spmd.sunk | while | flops 210861056 | bytes 10283621 | solution.py:129
  42.3 5.3 while.52
  55.4 135.6 %collective-permute-done = f32[2048,768]{1,0:T(8,128)} collective-permute-done((f32[2048,768]{1,0:T(8,128)S(1)}, f32[2048,768]{1,0:T(8,128)}, u32[]{:S(2)}, u32[]{:S(2)}) %collective-permute-start) | collective-permute-done | bytes 6291488 | tf_op jit(solution)/shard_map/ppermute | solution.py:138
  191.0 4.1 add.158
  198.0 269.5 %collective-permute-done.1 = f32[2048,768]{1,0:T(8,128)S(1)} collective-permute-done((f32[2048,768]{1,0:T(8,128)S(1)}, f32[2048,768]{1,0:T(8,128)S(1)}, u32[]{:S(2)}, u32[]{:S(2)}) %collective-permute-start.1) | collective-permute-done | bytes 6291488 | tf_op jit(solution)/shard_map/ppermute | solution.py:138
  471.6 18.4 %multiply_convert_fusion.2 = (bf16[2048,768]{1,0:T(8,128)(2,1)S(1)}, f32[2048,768]{1,0:T(8,128)}, f32[2048,768]{1,0:T(8,128)}) fusion(f32[768]{0:T(1024)S(1)} %convert_reduce_fusion.3, bf16[2048,768]{1,0:T(8,128)(2,1)S(1)} %fusion.103, bf16[768,768]{1,0:T(8,128)(2,1)S(1)} %copy-done), kind=kOutput, calls=%fused_computation.132 | convolution fusion | flops 2519728128 | bytes 20057088 | tf_op jit(solution)/shard_map/dot_general | solution.py:144
  491.7 4.7 fusion.138
  496.5 224.0 %all-reduce.5.cloned.1.call-done = f32[2048,768]{1,0:T(8,128)} async-done(((f32[2048,768]{1,0:T(8,128)}), f32[2048,768]{1,0:T(8,128)}) %all-reduce.5.cloned.1.call-update) | async-done | bytes 6291472 | tf_op jit(solution)/shard_map/psum | solution.py:149
  720.5 5.7 fusion.128
  732.1 5.3 fusion.126
  737.4 9.0 convert_reduce_fusion.1
  748.1 4.5 fusion.139
  754.9 219.7 %all-reduce.7.cloned.1.call-done = f32[2048,768]{1,0:T(8,128)} async-done(((f32[2048,768]{1,0:T(8,128)}), f32[2048,768]{1,0:T(8,128)}) %all-reduce.7.cloned.1.call-update) | async-done | bytes 6291472 | tf_op jit(solution)/shard_map/psum | solution.py:179
  974.6 8.3 multiply_reduce_fusion.2
  983.0 4.7 fusion.125
  996.0 25.9 %while.55 = (s32[]{:T(128)}, bf16[3,512,3,64]{1,3,2,0:T(8,128)(2,1)}, bf16[3,512,3,64]{1,3,2,0:T(8,128)(2,1)}, bf16[3,512,3,64]{1,3,2,0:T(8,128)(2,1)}, bf16[3,5...) while((s32[]{:T(128)}, ...), condition=%wide.region_23.24_spmd, body=%wide.region_21.23_spmd.sunk | while | flops 510589952 | bytes 35625200 | solution.py:201
  1022.9 5.1 fusion.119
  1028.2 9.9 while.54
  1049.1 5.0 fusion.116
  1054.2 4.2 copy.129
  1058.4 4.7 reshape.242
  1063.1 6.0 convolution_bitcast_fusion.1
  1069.2 8.0 fusion.110
  1077.6 7.0 fusion.140
  1094.9 13.4 all-reduce
  1111.9 10.3 reduce-scatter.25.cloned.1.call-done
  1123.8 42.0 %reduce-scatter.23.cloned.1.call-done = f32[96,576]{1,0:T(8,128)} async-done(((f32[768,576]{1,0:T(8,128)}), f32[96,576]{1,0:T(8,128)}) %reduce-scatter.23.cloned.1.call-update) | async-done | bytes 221200
  1167.7 223.4 %all-reduce.9.cloned.1.call-done = f32[2048,768]{1,0:T(8,128)} async-done(((f32[2048,768]{1,0:T(8,128)}), f32[2048,768]{1,0:T(8,128)}) %all-reduce.9.cloned.1.call-update) | async-done | bytes 6291472 | tf_op jit(solution)/shard_map/psum | solution.py:230
  1391.0 5.5 add.181
  1400.3 36.0 %reduce-scatter.21.cloned.1.call-done = f32[768,96]{0,1:T(8,128)} async-done(((f32[768,768]{0,1:T(8,128)}), f32[768,96]{0,1:T(8,128)}) %reduce-scatter.21.cloned.1.call-update) | async-done | bytes 294928 | tf_op jit(solution)/shard_map/reduce_scatter | solution.py:175
  1436.3 46.2 %reduce-scatter.19.cloned.1.call-done = f32[96,768]{1,0:T(8,128)} async-done(((f32[768,768]{1,0:T(8,128)}), f32[96,768]{1,0:T(8,128)}) %reduce-scatter.19.cloned.1.call-update) | async-done | bytes 294928 | tf_op jit(solution)/shard_map/reduce_scatter | solution.py:174
  (314 shorter events, 138.5 us)
Async XLA Ops:
  7.2 464.4 %copy-start = (bf16[768,768]{1,0:T(8,128)(2,1)S(1)}, bf16[768,768]{1,0:T(8,128)(2,1)}, u32[]{:S(2)}) copy-start(bf16[768,768]{1,0:T(8,128)(2,1)} %param.33) | copy-start | bytes 3538948
  7.2 713.3 %all-reduce.5.cloned.1.call-start = ((), (), s32[]{:S(2)}) async-start(), calls=%async_computation.7 | async-start | bytes 12582912 | tf_op jit(solution)/shard_map/psum | solution.py:149
  12.8 8.2 copy-start.34
  21.0 17.8 %copy-start.21 = (bf16[1,512,192]{1,2,0:T(8,128)(2,1)S(1)}, bf16[1,512,192]{1,2,0:T(8,128)(2,1)}, u32[]{:S(2)}) copy-start(bf16[1,512,192]{1,2,0:T(8,128)(2,1)} %get-tuple-element.457) | copy-start | bytes 589828
  21.0 19.5 %copy-start.20 = (bf16[1,512,192]{1,2,0:T(8,128)(2,1)S(1)}, bf16[1,512,192]{1,2,0:T(8,128)(2,1)}, u32[]{:S(2)}) copy-start(bf16[1,512,192]{1,2,0:T(8,128)(2,1)} %get-tuple-element.456) | copy-start | bytes 589828
  21.0 21.1 %copy-start.19 = (bf16[1,512,192]{1,2,0:T(8,128)(2,1)S(1)}, bf16[1,512,192]{1,2,0:T(8,128)(2,1)}, u32[]{:S(2)}) copy-start(bf16[1,512,192]{1,2,0:T(8,128)(2,1)} %get-tuple-element.455) | copy-start | bytes 589828
  21.1 21.2 %copy-start.35 = (s32[2]{0:T(128)S(1)}, s32[2]{0:T(128)}, u32[]{:S(2)}) copy-start(s32[2]{0:T(128)} %param.24) | copy-start | bytes 28
  52.2 145.7 %copy-start.29 = (bf16[2,768]{1,0:T(2,128)(2,1)S(1)}, bf16[2,768]{1,0:T(2,128)(2,1)}, u32[]{:S(2)}) copy-start(bf16[2,768]{1,0:T(2,128)(2,1)} %param.30) | copy-start | bytes 9220
  52.2 145.7 %copy-start.30 = (bf16[2,768]{1,0:T(2,128)(2,1)S(1)}, bf16[2,768]{1,0:T(2,128)(2,1)}, u32[]{:S(2)}) copy-start(bf16[2,768]{1,0:T(2,128)(2,1)} %param.31) | copy-start | bytes 9220
  52.2 145.7 %copy-start.31 = (bf16[2,768]{1,0:T(2,128)(2,1)S(1)}, bf16[2,768]{1,0:T(2,128)(2,1)}, u32[]{:S(2)}) copy-start(bf16[2,768]{1,0:T(2,128)(2,1)} %param.32) | copy-start | bytes 9220
  52.2 145.7 %copy-start.28 = (bf16[1,768]{1,0:T(2,128)(2,1)S(1)}, bf16[1,768]{1,0:T(2,128)(2,1)}, u32[]{:S(2)}) copy-start(bf16[1,768]{1,0:T(2,128)(2,1)} %param.34) | copy-start | bytes 4612
  52.2 415.3 %copy-start.16 = (bf16[3,512,768]{2,1,0:T(8,128)(2,1)S(1)}, bf16[3,512,768]{2,1,0:T(8,128)(2,1)}, u32[]{:S(2)}) copy-start(bf16[3,512,768]{2,1,0:T(8,128)(2,1)} %param.25) | copy-start | bytes 7077892
  52.2 415.3 %copy-start.18 = (bf16[2,256,768]{2,1,0:T(8,128)(2,1)S(1)}, bf16[2,256,768]{2,1,0:T(8,128)(2,1)}, u32[]{:S(2)}) copy-start(bf16[2,256,768]{2,1,0:T(8,128)(2,1)} %param.23) | copy-start | bytes 2359300
  52.2 138.7 %collective-permute-start = (f32[2048,768]{1,0:T(8,128)S(1)}, f32[2048,768]{1,0:T(8,128)}, u32[]{:S(2)}, u32[]{:S(2)}) collective-permute-start(f32[2048,768]{1,0:T(8,128)S(1)} %fusion.137), channel_id=1, source_target_pairs={{0,1},{1,0},{2,3},{3,2},{4,5},{5,4},{6,7},{7,6},{8,9},{9,8},{10,11... | collective-permute-start | bytes 18874376 | tf_op jit(solution)/shard_map/ppermute | solution.py:138
  195.1 272.5 %collective-permute-start.1 = (f32[2048,768]{1,0:T(8,128)S(1)}, f32[2048,768]{1,0:T(8,128)S(1)}, u32[]{:S(2)}, u32[]{:S(2)}) collective-permute-start(f32[2048,768]{1,0:T(8,128)S(1)} %add.158), channel_id=1, source_target_pairs={{0,2},{1,3},{2,0},{3,1},{4,6},{5,7},{6,4},{7,5},{8,10},{9,11},{10,... | collective-permute-start | bytes 18874376 | tf_op jit(solution)/shard_map/ppermute | solution.py:138
  471.6 18.4 %copy-start.13 = (bf16[2048,768]{1,0:T(8,128)(2,1)}, bf16[2048,768]{1,0:T(8,128)(2,1)S(1)}, u32[]{:S(2)}) copy-start(bf16[2048,768]{1,0:T(8,128)(2,1)S(1)} %fusion.103) | copy-start | bytes 9437188
  471.6 20.2 %copy-start.32 = (bf16[768,768]{1,0:T(8,128)(2,1)S(1)}, bf16[768,768]{1,0:T(8,128)(2,1)}, u32[]{:S(2)}) copy-start(bf16[768,768]{1,0:T(8,128)(2,1)} %param.35) | copy-start | bytes 3538948
  496.5 478.1 %all-reduce.7.cloned.1.call-start = ((), (), s32[]{:S(2)}) async-start(), calls=%async_computation.8 | async-start | bytes 12582912 | tf_op jit(solution)/shard_map/psum | solution.py:179
  728.1 9.3 slice-start.1
  737.4 9.0 copy-start.4
  752.7 338.4 %reduce-scatter.31.cloned.1.call-start = ((), (), s32[]{:S(2)}) async-start(), calls=%async_computation.16 | async-start | bytes 442368
  753.8 338.7 %reduce-scatter.29.cloned.1.call-start = ((), (), s32[]{:S(2)}) async-start(), calls=%async_computation.15 | async-start | bytes 442368
  754.8 354.1 %reduce-scatter.27.cloned.1.call-start = ((), (), s32[]{:S(2)}) async-start(), calls=%async_computation.14 | async-start | bytes 442368
  982.9 7.4 copy-start.17
  1021.8 6.3 copy-start.27
  1022.8 99.4 %reduce-scatter.25.cloned.1.call-start = ((), (), s32[]{:S(2)}) async-start(), calls=%async_computation.13 | async-start | bytes 884736
  1028.1 137.7 %reduce-scatter.23.cloned.1.call-start = ((), (), s32[]{:S(2)}) async-start(), calls=%async_computation.12 | async-start | bytes 2211840
  1063.1 328.0 %all-reduce.9.cloned.1.call-start = ((), (), s32[]{:S(2)}) async-start(), calls=%async_computation.9 | async-start | bytes 12582912 | tf_op jit(solution)/shard_map/psum | solution.py:230
  1069.1 367.1 %reduce-scatter.21.cloned.1.call-start = ((), (), s32[]{:S(2)}) async-start(), calls=%async_computation.11 | async-start | bytes 2654208 | tf_op jit(solution)/shard_map/reduce_scatter | solution.py:175
  1077.2 7.3 copy-start.37
  1077.2 405.2 %reduce-scatter.19.cloned.1.call-start = ((), (), s32[]{:S(2)}) async-start(), calls=%async_computation.10 | async-start | bytes 2654208 | tf_op jit(solution)/shard_map/reduce_scatter | solution.py:174
  1391.0 91.4 %copy-start.1 = (bf16[768,768]{1,0:T(8,128)(2,1)S(1)}, bf16[768,768]{1,0:T(8,128)(2,1)}, u32[]{:S(2)}) copy-start(bf16[768,768]{1,0:T(8,128)(2,1)} %param.33) | copy-start | bytes 3538948
  (31 other events, 91.6 us)
Sparse Core Ops, SparseCore 0:
  496.6 223.8 all-reduce.4
  752.8 221.7 all-reduce.6
  977.7 32.7 reduce-scatter.30
  1013.4 33.9 reduce-scatter.28
  1050.2 33.8 reduce-scatter.26
  1087.2 34.9 reduce-scatter.24
  1125.6 40.1 reduce-scatter.22
  1168.2 222.8 all-reduce.8
  1395.0 41.2 reduce-scatter.20
  1440.0 42.3 reduce-scatter.18
